TPU v7x, 512 devices: a whole 4x8x8 slice. The times are simulated.
512 devices in a mesh: coil: 32 (over x, y), slab: 16 (over z, core).
Axes of the slice: x: 4, y: 8, z: 8, core: 2. Of those that a mesh axis runs over, the one named last changes fastest.
Arguments:
- adjoint_data: float32 [16, 192, 384], P('slab', 'coil'), may hold values from -80 to 80
- denoised: float32 [16, 192, 384], P('slab', 'coil'), may hold values from -8 to 8, as said below
- sensitivity: float32 [32, 16, 192, 384], P('coil', 'slab'), may hold values from -2 to 2, as said below
- kernel: float32 [16, 384, 384], P(None, 'slab'), may hold values from 0.1 to 2, as said below
- conv_in: bfloat16 [54, 64], replicated, may hold values from -0.875 to 0.875
- conv_mid: bfloat16 [1728, 64], replicated, may hold values from -0.15625 to 0.15625
- conv_out: bfloat16 [1728, 2], replicated, may hold values from -0.15625 to 0.15625
Outputs:
- solution: float32 [16, 192, 384], P('slab', 'coil')
- refined: float32 [16, 192, 384], P('slab', 'coil')
Inputs may be any that keep to these rules, and one draw needn't show every extreme that they name: `denoised`: real and imaginary parts of the previous cascade's image. `sensitivity`: real and imaginary parts of the coil maps. Positive kernel values.
All inputs are finite; a program needn't handle non-finite values.
Results may differ from a plain program's by a relative error of at most 0.0023.
Values may be sent and summed in bfloat16 or wider, within the bound.
A program may use at most 64 MiB of HBM per device.

v0:
```python
import math
import jax
import jax.numpy as jnp
from jax import lax
from jax.sharding import PartitionSpec as P

ITERS = 2
reg_weight = 0.5
highest = lax.Precision.HIGHEST


def with_halo(cells, sides, width):
    for axis, dim in sides:
        count = lax.axis_size(axis)
        ends = count - 1
        head = lax.slice_in_dim(cells, 0, width, axis=dim)
        tail = lax.slice_in_dim(cells, cells.shape[dim] - width, cells.shape[dim], axis=dim)
        cells = jnp.concatenate(
            [
                lax.ppermute(tail, axis, [(i, (i + 1) % count) for i in range(ends)]),
                cells,
                lax.ppermute(head, axis, [((i + 1) % count, i) for i in range(ends)]),
            ],
            axis=dim,
        )
    return cells


def dft_tables(out_len, in_len, length, inverse):
    out_index = lax.broadcasted_iota(jnp.int32, (out_len, in_len), 0)
    in_index = lax.broadcasted_iota(jnp.int32, (out_len, in_len), 1)
    phases = (out_index * in_index % length).astype(jnp.float32) * (2.0 * math.pi / length)
    if inverse:
        return (jnp.cos(phases) / length, jnp.sin(phases) / length)
    return (jnp.cos(phases), -jnp.sin(phases))


def block_matrix(tables):
    cos_table = tables[0]
    sin_table = tables[1]
    upper = jnp.concatenate([cos_table.T, sin_table.T], axis=1)
    lower = jnp.concatenate([-sin_table.T, cos_table.T], axis=1)
    return jnp.concatenate([upper, lower], axis=0)


def along_axis(values, tables, einsum_form):
    half_len = values.shape[-1] // 2
    real_part = jnp.einsum(einsum_form, tables[0], values, precision=highest)
    imag_part = jnp.einsum(einsum_form, tables[1], values, precision=highest)
    return jnp.concatenate(
        [
            real_part[..., :half_len] - imag_part[..., half_len:],
            real_part[..., half_len:] + imag_part[..., :half_len],
        ],
        axis=-1,
    )


def complex_product(factor_one, factor_two):
    half_len = factor_one.shape[-1] // 2
    real_one = factor_one[..., :half_len]
    imag_one = factor_one[..., half_len:]
    real_two = factor_two[..., :half_len]
    imag_two = factor_two[..., half_len:]
    return jnp.concatenate(
        [real_one * real_two - imag_one * imag_two, real_one * imag_two + imag_one * real_two],
        axis=-1,
    )


def conj_product(factor_one, factor_two):
    half_len = factor_one.shape[-1] // 2
    real_one = factor_one[..., :half_len]
    imag_one = factor_one[..., half_len:]
    real_two = factor_two[..., :half_len]
    imag_two = factor_two[..., half_len:]
    return jnp.concatenate(
        [real_one * real_two + imag_one * imag_two, real_one * imag_two - imag_one * real_two],
        axis=-1,
    )


def convolve(features, weights, in_channels):
    padded = with_halo(features, (("coil", 1), ("slab", 0)), 1)
    depth_here = features.shape[0]
    rows_here = features.shape[1]
    side_len = features.shape[2] // in_channels
    padded_cube = padded.reshape(depth_here + 2, rows_here + 2, side_len, in_channels)
    padded_cube = jnp.pad(padded_cube, ((0, 0), (0, 0), (1, 1), (0, 0)))
    width_taps = 9 * in_channels
    running = None
    for shift_z in range(3):
        tap_list = [
            padded_cube[
                shift_z : shift_z + depth_here,
                shift_x : shift_x + rows_here,
                shift_y : shift_y + side_len,
                :,
            ]
            for shift_x in range(3)
            for shift_y in range(3)
        ]
        patches = jnp.concatenate(tap_list, axis=-1).reshape(-1, width_taps)
        partial_sum = jnp.dot(
            patches,
            weights[shift_z * width_taps : (shift_z + 1) * width_taps],
            preferred_element_type=jnp.float32,
        )
        running = partial_sum if shift_z == 0 else running + partial_sum
    return running


def shards(adjoint_data, denoised, sensitivity, kernel, conv_in, conv_mid, conv_out):
    side_len = sensitivity.shape[2]
    depth_len = kernel.shape[0]
    grid_len = kernel.shape[2]
    fwd_plane = dft_tables(grid_len, side_len, grid_len, False)
    inv_plane = dft_tables(side_len, grid_len, grid_len, True)
    fwd_depth = dft_tables(depth_len, depth_len, depth_len, False)
    inv_depth = dft_tables(depth_len, depth_len, depth_len, True)
    fwd_last = block_matrix(fwd_plane)
    inv_last = block_matrix(inv_plane)

    def total_squares(residual):
        return lax.psum(jnp.sum(residual * residual), ("coil", "slab"))

    right_side = adjoint_data + reg_weight * denoised
    solution = jnp.zeros_like(right_side)
    residual = right_side
    direction = right_side
    norm_now = total_squares(residual)
    for iteration in range(ITERS):
        products = complex_product(
            sensitivity, lax.all_gather(direction, "coil", axis=1, tiled=True)[None]
        )
        products = jnp.matmul(products, fwd_last, precision=highest)
        spread = along_axis(products, fwd_plane, "kn,cznw->czkw")
        apply_pencil = lax.all_to_all(spread, "slab", split_axis=2, concat_axis=1, tiled=True)
        spectrum = along_axis(apply_pencil, fwd_depth, "kn,cnxw->ckxw")
        shape_now = spectrum.shape
        split_form = spectrum.reshape(shape_now[0], shape_now[1], shape_now[2], 2, grid_len)
        weighted = split_form * kernel[None, :, :, None, :]
        returned = along_axis(weighted.reshape(shape_now), inv_depth, "kn,cnxw->ckxw")
        slab_back = lax.all_to_all(returned, "slab", split_axis=1, concat_axis=2, tiled=True)
        image_back = along_axis(slab_back, inv_plane, "kn,cznw->czkw")
        image_back = jnp.matmul(image_back, inv_last, precision=highest)
        coil_sum = jnp.sum(conj_product(sensitivity, image_back), axis=0)
        summed = lax.psum_scatter(coil_sum, "coil", scatter_dimension=1, tiled=True)
        image_out = summed + reg_weight * direction
        local_curv = jnp.sum(direction * image_out)
        image_out, local_curv = (image_out, local_curv)
        curvature = lax.psum(local_curv, ("coil", "slab"))
        step_size = norm_now / curvature
        solution = solution + step_size * direction
        if iteration + 1 < ITERS:
            residual = residual - step_size * image_out
            norm_next = total_squares(residual)
            direction = residual + norm_next / norm_now * direction
            norm_now = norm_next
    depth_here = solution.shape[0]
    rows_here = solution.shape[1]
    channels = jnp.stack([solution[..., :side_len], solution[..., side_len:]], axis=-1).astype(
        jnp.bfloat16
    )
    first_map = convolve(channels.reshape(depth_here, rows_here, 2 * side_len), conv_in, 2)
    hidden_count = conv_mid.shape[1]
    hidden_one = (
        jax.nn.relu(first_map)
        .astype(jnp.bfloat16)
        .reshape(depth_here, rows_here, side_len * hidden_count)
    )
    second_map = convolve(hidden_one, conv_mid, hidden_count)
    hidden_two = (
        jax.nn.relu(second_map)
        .astype(jnp.bfloat16)
        .reshape(depth_here, rows_here, side_len * hidden_count)
    )
    third_map = convolve(hidden_two, conv_out, hidden_count).reshape(
        depth_here, rows_here, side_len, 2
    )
    refined = solution + jnp.concatenate([third_map[..., 0], third_map[..., 1]], axis=-1)
    return (solution, refined)


def solution(mesh):
    placed = (
        P("slab", "coil", None),
        P("slab", "coil", None),
        P("coil", "slab", None, None),
        P(None, "slab", None),
        P(),
        P(),
        P(),
    )
    return jax.shard_map(
        shards,
        mesh=mesh,
        in_specs=placed,
        out_specs=(P("slab", "coil", None), P("slab", "coil", None)),
        check_vma=False,
    )
```

profile of v0, /device:TPU:249, one launch (start us, length us, event | category | flops | bytes accessed | tf_op | source)
XLA Modules:
  0.0 1028.2 jit_solution(9897725327793448658)
XLA Ops:
  10.4 37.1 %all_gather.6 = f32[1,192,384]{2,0,1:T(1,128)S(1)} all-gather(f32[1,6,384]{2,0,1:T(1,128)S(1)} %copy.111), channel_id=1, replica_groups=mesh['coil'=32,'slab'=16] {'coil'}, dimensions={1}, use_global_device_ids=true | all-gather | bytes 304128 | tf_op jit(solution)/shard_map/all_gather | solution.py:134
  48.9 4.0 convolution_bitcast_fusion.10
  52.9 4.0 convolution_bitcast_fusion.11
  57.1 2.7 copy.112
  59.8 21.2 %all-to-all-start = ((f32[1,1,384,768]{3,1,0,2:T(1,128)}), f32[1,1,384,768]{3,1,0,2:T(1,128)S(1)}, u32[]{:S(2)}, u32[]{:S(2)}) async-start(f32[1,1,384,768]{3,1,0,2:T(1,128)} %copy.112), calls=%async_computation | async-start | bytes 2359296 | tf_op jit(solution)/shard_map/all_to_all | solution.py:138
  81.2 1.7 mul.249
  82.9 2.2 mul.250
  85.1 25.0 %all-to-all-done = f32[1,1,384,768]{3,1,0,2:T(1,128)S(1)} async-done(((f32[1,1,384,768]{3,1,0,2:T(1,128)}), f32[1,1,384,768]{3,1,0,2:T(1,128)S(1)}, u32[]{:S(2)}, u32[]{:S(2)}) %all-to-all-start) | async-done | bytes 1179680 | tf_op jit(solution)/shard_map/all_to_all | solution.py:138
  115.9 1.7 copy.116
  117.6 5.2 all-to-all-start.1
  123.0 1.5 fusion.59
  124.5 2.4 fusion.25
  127.0 24.9 %all-to-all-done.1 = f32[1,16,24,768]{3,2,0,1:T(8,128)S(1)} async-done(((f32[1,16,24,768]{3,2,0,1:T(8,128)}), f32[1,16,24,768]{3,2,0,1:T(8,128)S(1)}, u32[]{:S(2)}, u32[]{:S(2)}) %all-to-all-start.1) | async-done | bytes 1179680 | tf_op jit(solution)/shard_map/all_to_all | solution.py:144
  151.8 2.3 convolution_bitcast_fusion.14
  154.1 2.3 convolution_bitcast_fusion.15
  162.2 145.9 %all-reduce.9.cloned.1.call-done = f32[1,192,384]{2,0,1:T(1,128)} async-done(((f32[1,192,384]{2,0,1:T(1,128)}), f32[1,192,384]{2,0,1:T(1,128)}) %all-reduce.9.cloned.1.call-update) | async-done | bytes 294928
  309.4 99.0 %all-reduce.5 = (f32[]{:T(128)}, f32[]{:T(128)}) all-reduce(f32[]{:T(128)} %get-tuple-element.13, f32[]{:T(128)} %get-tuple-element.12), channel_id=1, replica_groups=mesh['coil'=32,'slab'=16] {'coil','slab'}, use_global_device_ids=true, to_apply=%region_1.2 | all-reduce | flops 2 | bytes 16 | tf_op jit(solution)/shard_map/psum | solution.py:125
  410.4 94.7 %psum.30 = f32[]{:T(128)} all-reduce(f32[]{:T(128)} %multiply_reduce_fusion), channel_id=1, replica_groups=mesh['coil'=32,'slab'=16] {'coil','slab'}, use_global_device_ids=true, to_apply=%region_6.7 | all-reduce | flops 1 | bytes 8 | tf_op jit(solution)/shard_map/psum | solution.py:125
  506.5 37.2 %all_gather.7 = f32[1,192,384]{2,0,1:T(1,128)S(1)} all-gather(f32[1,6,384]{2,0,1:T(1,128)S(1)} %copy.119), channel_id=1, replica_groups=mesh['coil'=32,'slab'=16] {'coil'}, dimensions={1}, use_global_device_ids=true | all-gather | bytes 304128 | tf_op jit(solution)/shard_map/all_gather | solution.py:134
  545.1 4.0 convolution_bitcast_fusion.8
  549.1 4.0 convolution_bitcast_fusion.9
  553.3 2.7 copy.120
  556.0 47.3 %all_to_all.16 = f32[1,1,384,768]{3,1,0,2:T(1,128)S(1)} all-to-all(f32[1,1,384,768]{3,1,0,2:T(1,128)} %copy.120), channel_id=1, replica_groups=mesh['coil'=32,'slab'=16] {'slab'}, dimensions={2} | all-to-all | bytes 2359296 | tf_op jit(solution)/shard_map/all_to_all | solution.py:138
  604.9 1.4 convolution_bitcast_fusion.3
  609.9 34.2 %all_to_all.17 = f32[1,16,24,768]{3,2,0,1:T(8,128)S(1)} all-to-all(f32[1,16,24,768]{3,2,0,1:T(8,128)S(1)} %copy.123), channel_id=1, replica_groups=mesh['coil'=32,'slab'=16] {'slab'}, dimensions={1} | all-to-all | bytes 2359296 | tf_op jit(solution)/shard_map/all_to_all | solution.py:144
  644.1 2.3 convolution_bitcast_fusion.12
  646.4 2.3 convolution_bitcast_fusion.13
  652.4 148.8 %all-reduce.11.cloned.1.call-done = f32[1,192,384]{2,0,1:T(1,128)} async-done(((f32[1,192,384]{2,0,1:T(1,128)}), f32[1,192,384]{2,0,1:T(1,128)}) %all-reduce.11.cloned.1.call-update) | async-done | bytes 294928
  802.5 98.9 %psum.31 = f32[]{:T(128)} all-reduce(f32[]{:T(128)} %fusion.74), channel_id=1, replica_groups=mesh['coil'=32,'slab'=16] {'coil','slab'}, use_global_device_ids=true, to_apply=%region_9.10 | all-reduce | flops 1 | bytes 8 | tf_op jit(solution)/shard_map/psum | solution.py:152
  903.1 5.1 collective-permute-start
  908.2 1.9 collective-permute-start.1
  910.3 5.3 collective-permute-done.1
  915.8 4.0 collective-permute-start.3
  919.8 3.5 collective-permute-start.2
  924.0 1.5 fusion.193
  925.5 1.6 fusion.192
  927.2 4.2 concatenate.143
  932.1 1.7 concatenate.142
  934.6 1.7 concatenate.141
  938.3 1.9 collective-permute-start.4
  940.3 3.4 collective-permute-start.5
  943.7 3.6 collective-permute-done.5
  947.4 4.0 collective-permute-start.7
  951.4 4.7 collective-permute-start.6
  961.2 1.7 pad_slice_fusion.18
  962.9 2.0 pad_slice_fusion.19
  964.8 3.1 concatenate.146
  967.9 2.2 fusion.71
  970.1 2.7 concatenate.147
  972.8 2.4 convolution_add_fusion.1
  975.2 2.9 concatenate.148
  978.1 1.5 fusion.3
  980.2 1.9 collective-permute-start.8
  982.1 3.4 collective-permute-start.9
  985.5 4.0 collective-permute-done.9
  989.6 2.7 collective-permute-start.11
  992.3 5.5 collective-permute-start.10
  1003.2 1.7 pad_slice_fusion
  1004.9 2.0 pad_slice_fusion.1
  1006.8 3.1 concatenate.151
  1009.9 1.8 fusion.115
  1011.7 2.7 concatenate.152
  1014.4 1.8 convolution_add_fusion.5
  1016.2 2.9 concatenate.153
  (128 shorter events, 47.5 us)
Async XLA Ops:
  7.2 40.4 %copy-start = (f32[1,1,192,384]{3,2,1,0:T(8,128)S(1)}, f32[1,1,192,384]{3,2,1,0:T(8,128)}, u32[]{:S(2)}) copy-start(f32[1,1,192,384]{3,2,1,0:T(8,128)} %param.9) | copy-start | bytes 884740
  8.3 39.4 %copy-start.5 = (f32[192,384]{1,0:T(8,128)}, f32[192,384]{1,0:T(8,128)S(1)}, u32[]{:S(2)}) copy-start(f32[192,384]{1,0:T(8,128)S(1)} %fusion.66) | copy-start | bytes 884740
  9.5 39.4 %copy-start.7 = (f32[192,384]{1,0:T(8,128)}, f32[192,384]{1,0:T(8,128)S(1)}, u32[]{:S(2)}) copy-start(f32[192,384]{1,0:T(8,128)S(1)} %get-tuple-element.133) | copy-start | bytes 884740
  9.5 39.4 %copy-start.9 = (f32[192,384]{1,0:T(8,128)}, f32[192,384]{1,0:T(8,128)S(1)}, u32[]{:S(2)}) copy-start(f32[192,384]{1,0:T(8,128)S(1)} %get-tuple-element.134) | copy-start | bytes 884740
  59.8 21.2 %copy-start.2 = (f32[16,24,384]{2,1,0:T(8,128)S(1)}, f32[16,24,384]{2,1,0:T(8,128)}, u32[]{:S(2)}) copy-start(f32[16,24,384]{2,1,0:T(8,128)} %param.10) | copy-start | bytes 1769476
  59.8 50.2 %all-to-all-start = ((f32[1,1,384,768]{3,1,0,2:T(1,128)}), f32[1,1,384,768]{3,1,0,2:T(1,128)S(1)}, u32[]{:S(2)}, u32[]{:S(2)}) async-start(f32[1,1,384,768]{3,1,0,2:T(1,128)} %copy.112), calls=%async_computation | async-start | bytes 2359296 | tf_op jit(solution)/shard_map/all_to_all | solution.py:138
  117.6 34.2 %all-to-all-start.1 = ((f32[1,16,24,768]{3,2,0,1:T(8,128)}), f32[1,16,24,768]{3,2,0,1:T(8,128)S(1)}, u32[]{:S(2)}, u32[]{:S(2)}) async-start(f32[1,16,24,768]{3,2,0,1:T(8,128)} %copy.116), calls=%async_computation.1 | async-start | bytes 2359296 | tf_op jit(solution)/shard_map/all_to_all | solution.py:144
  122.8 185.3 %all-reduce.9.cloned.1.call-start = ((), (), s32[]{:S(2)}) async-start(), calls=%async_computation.4 | async-start | bytes 589824
  156.5 1.0 copy-start.3
  160.1 383.8 %copy-start.6 = (f32[192,384]{1,0:T(8,128)S(1)}, f32[192,384]{1,0:T(8,128)}, u32[]{:S(2)}) copy-start(f32[192,384]{1,0:T(8,128)} %copy-done.5) | copy-start | bytes 884740
  160.1 383.8 %copy-start.8 = (f32[192,384]{1,0:T(8,128)S(1)}, f32[192,384]{1,0:T(8,128)}, u32[]{:S(2)}) copy-start(f32[192,384]{1,0:T(8,128)} %copy-done.7) | copy-start | bytes 884740
  160.2 383.8 %copy-start.10 = (f32[192,384]{1,0:T(8,128)S(1)}, f32[192,384]{1,0:T(8,128)}, u32[]{:S(2)}) copy-start(f32[192,384]{1,0:T(8,128)} %copy-done.9) | copy-start | bytes 884740
  160.2 641.0 %all-reduce.11.cloned.1.call-start = ((), (), s32[]{:S(2)}) async-start(), calls=%async_computation.5 | async-start | bytes 589824
  648.8 1.0 copy-start.4
  903.1 7.1 collective-permute-start
  908.2 7.5 collective-permute-start.1
  915.8 7.5 collective-permute-start.3
  919.8 4.0 collective-permute-start.2
  936.2 0.8 copy-start.12
  938.3 5.3 collective-permute-start.4
  940.3 6.9 collective-permute-start.5
  947.4 9.9 collective-permute-start.7
  951.4 7.1 collective-permute-start.6
  975.2 2.9 copy-start.1
  980.2 5.3 collective-permute-start.8
  982.1 7.4 collective-permute-start.9
  989.6 9.7 collective-permute-start.11
  992.3 8.1 collective-permute-start.10
  1016.2 2.9 copy-start.11
Sparse Core Ops, SparseCore 0:
  160.3 147.8 all-reduce.8
  652.5 148.5 all-reduce.10
where the time goes:
time: 1030 us
  blocking collectives  449 us (44%)
  waiting for transfers between devices  362 us (35%)
  starting transfers between devices  68.6 us (7%)
  local copies, waits for them, and re-layouts  64.6 us (6%)
  matrix products  52.4 us (5%)
  between operations  19.8 us (2%)
  other arithmetic  12 us (1%)
    unnamed x4, waiting for transfers between devices  295 us
    psum x2, blocking collectives, total_squares(): return lax.psum(jnp.sum(residual * residual), ('coil', 'slab'))  194 us
    psum x1, blocking collectives, shards(): curvature = lax.psum(local_curv, ('coil', 'slab'))  98.9 us
    all_gather x2, blocking collectives, shards(): lax.all_gather(direction, 'coil', axis=1, tiled=True)[None]  74.3 us
    all_to_all x1, blocking collectives, shards(): lax.all_to_all(spread, 'slab', split_axis=2, concat_axis=1, tiled=True)  47.3 us
    all_to_all x1, blocking collectives, shards(): lax.all_to_all(returned, 'slab', split_axis=1, concat_axis=2, tiled=True)  34.2 us
    concatenate x12, local copies, waits for them, and re-layouts, convolve(): patches = jnp.concatenate(tap_list, axis=-1).reshape(-1, width_taps)  26.8 us
    all_to_all x1, waiting for transfers between devices, shards(): lax.all_to_all(spread, 'slab', split_axis=2, concat_axis=1, tiled=True)  25 us
  transfers between devices with their start and end apart: 16, of which 12 were waited for; matrix products, arithmetic and copies ran while one was open for 1% of the time, Pallas kernels for 0%

commit v1 on v0

--- a/solution.py
+++ b/solution.py
@@ -7,6 +7,13 @@
 ITERS = 2
 reg_weight = 0.5
 highest = lax.Precision.HIGHEST
+
+
+def all_by_exchange(x, axis, dim):
+    devices = lax.axis_size(axis)
+    shards = jnp.stack([x for _ in range(devices)])
+    shards = lax.all_to_all(shards, axis, split_axis=0, concat_axis=0)
+    return jnp.concatenate(shards, axis=dim)
 
 
 def with_halo(cells, sides, width):
@@ -130,9 +137,7 @@
     direction = right_side
     norm_now = total_squares(residual)
     for iteration in range(ITERS):
-        products = complex_product(
-            sensitivity, lax.all_gather(direction, "coil", axis=1, tiled=True)[None]
-        )
+        products = complex_product(sensitivity, all_by_exchange(direction, "coil", 1)[None])
         products = jnp.matmul(products, fwd_last, precision=highest)
         spread = along_axis(products, fwd_plane, "kn,cznw->czkw")
         apply_pencil = lax.all_to_all(spread, "slab", split_axis=2, concat_axis=1, tiled=True)

time: 1030 us -> 978 us (0.950)
  blocking collectives: 449 us -> 382 us
    all_gather x2 -> x0, blocking collectives: 74.3 us -> none  [shards(): lax.all_gather(direction, 'coil', axis=1, tiled=True)[None]]
    all_to_all x0 -> x1, blocking collectives: none -> 18.3 us  [all_by_exchange(): shards = lax.all_to_all(shards, axis, split_axis=0, concat_axis=0)]
    all_to_all x1, starting transfers between devices: 21.2 us -> 10.4 us  [shards(): lax.all_to_all(spread, 'slab', split_axis=2, concat_axis=1, tiled=True)]
    all_to_all x1, blocking collectives: 47.3 us -> 36.9 us  [shards(): lax.all_to_all(spread, 'slab', split_axis=2, concat_axis=1, tiled=True)]
  transfers between devices with their start and end apart: 16 -> 17, of which waited for: 12 -> 13; matrix products, arithmetic and copies ran while one was open for 1% -> 1% of each run, Pallas kernels for 0% -> 0%
where the time goes in v1:
time: 978 us; the launch traced here: 967 us
  blocking collectives  382 us (39%)
  waiting for transfers between devices  367 us (38%)
  starting transfers between devices  66.6 us (7%)
  local copies, waits for them, and re-layouts  66.4 us (7%)
  matrix products  52.6 us (5%)
  between operations  20.1 us (2%)
  other arithmetic  12 us (1%)
    unnamed x4, waiting for transfers between devices  293 us
    psum x2, blocking collectives, total_squares(): return lax.psum(jnp.sum(residual * residual), ('coil', 'slab'))  194 us
    psum x1, blocking collectives, shards(): curvature = lax.psum(local_curv, ('coil', 'slab'))  98.9 us
    all_to_all x1, blocking collectives, shards(): lax.all_to_all(spread, 'slab', split_axis=2, concat_axis=1, tiled=True)  36.9 us
    all_to_all x1, blocking collectives, shards(): lax.all_to_all(returned, 'slab', split_axis=1, concat_axis=2, tiled=True)  34.2 us
    concatenate x12, local copies, waits for them, and re-layouts, convolve(): patches = jnp.concatenate(tap_list, axis=-1).reshape(-1, width_taps)  26.7 us
    all_to_all x1, waiting for transfers between devices, shards(): lax.all_to_all(spread, 'slab', split_axis=2, concat_axis=1, tiled=True)  25 us
    all_to_all x1, waiting for transfers between devices, shards(): lax.all_to_all(returned, 'slab', split_axis=1, concat_axis=2, tiled=True)  24.8 us
  transfers between devices with their start and end apart: 17, of which 13 were waited for; matrix products, arithmetic and copies ran while one was open for 1% of the time, Pallas kernels for 0%

profile of v1, /device:TPU:249, one launch (start us, length us, event | category | flops | bytes accessed | tf_op | source)
XLA Modules:
  0.0 967.0 jit_solution(10580463897557781071)
XLA Ops:
  8.8 9.1 all-to-all-start
  20.2 6.6 all-to-all-done
  28.6 4.0 convolution_bitcast_fusion.10
  32.6 4.1 convolution_bitcast_fusion.11
  37.0 2.7 copy.123
  39.7 10.4 %all-to-all-start.1 = ((f32[1,1,384,768]{3,1,0,2:T(1,128)}), f32[1,1,384,768]{3,1,0,2:T(1,128)S(1)}, u32[]{:S(2)}, u32[]{:S(2)}) async-start(f32[1,1,384,768]{3,1,0,2:T(1,128)} %copy.123), calls=%async_computation.1 | async-start | bytes 2359296 | tf_op jit(solution)/shard_map/all_to_all | solution.py:143
  50.2 1.7 mul.249
  51.9 2.2 mul.250
  54.1 25.0 %all-to-all-done.1 = f32[1,1,384,768]{3,1,0,2:T(1,128)S(1)} async-done(((f32[1,1,384,768]{3,1,0,2:T(1,128)}), f32[1,1,384,768]{3,1,0,2:T(1,128)S(1)}, u32[]{:S(2)}, u32[]{:S(2)}) %all-to-all-start.1) | async-done | bytes 1179680 | tf_op jit(solution)/shard_map/all_to_all | solution.py:143
  85.0 1.7 copy.127
  86.7 5.2 all-to-all-start.2
  92.0 1.5 fusion.59
  93.5 2.6 fusion.25
  96.1 24.8 %all-to-all-done.2 = f32[1,16,24,768]{3,2,0,1:T(8,128)S(1)} async-done(((f32[1,16,24,768]{3,2,0,1:T(8,128)}), f32[1,16,24,768]{3,2,0,1:T(8,128)S(1)}, u32[]{:S(2)}, u32[]{:S(2)}) %all-to-all-start.2) | async-done | bytes 1179680 | tf_op jit(solution)/shard_map/all_to_all | solution.py:149
  120.9 2.3 convolution_bitcast_fusion.14
  123.3 2.3 convolution_bitcast_fusion.15
  131.2 145.5 %all-reduce.9.cloned.1.call-done = f32[1,192,384]{2,0,1:T(1,128)} async-done(((f32[1,192,384]{2,0,1:T(1,128)}), f32[1,192,384]{2,0,1:T(1,128)}) %all-reduce.9.cloned.1.call-update) | async-done | bytes 294928
  278.0 99.0 %all-reduce.5 = (f32[]{:T(128)}, f32[]{:T(128)}) all-reduce(f32[]{:T(128)} %get-tuple-element.13, f32[]{:T(128)} %get-tuple-element.12), channel_id=1, replica_groups=mesh['coil'=32,'slab'=16] {'coil','slab'}, use_global_device_ids=true, to_apply=%region_1.2 | all-reduce | flops 2 | bytes 16 | tf_op jit(solution)/shard_map/psum | solution.py:132
  379.0 94.7 %psum.30 = f32[]{:T(128)} all-reduce(f32[]{:T(128)} %multiply_reduce_fusion), channel_id=1, replica_groups=mesh['coil'=32,'slab'=16] {'coil','slab'}, use_global_device_ids=true, to_apply=%region_6.7 | all-reduce | flops 1 | bytes 8 | tf_op jit(solution)/shard_map/psum | solution.py:132
  475.3 18.3 %all_to_all.46 = f32[32,1,6,384]{3,1,2,0:T(1,128)S(1)} all-to-all(f32[32,1,6,384]{3,1,2,0:T(1,128)S(1)} %stack.11), channel_id=1, replica_groups=mesh['coil'=32,'slab'=16] {'coil'}, dimensions={0} | all-to-all | bytes 589824 | tf_op jit(solution)/shard_map/all_to_all | solution.py:15
  495.4 4.0 convolution_bitcast_fusion.8
  499.4 4.0 convolution_bitcast_fusion.9
  503.6 2.7 copy.132
  506.3 36.9 %all_to_all.47 = f32[1,1,384,768]{3,1,0,2:T(1,128)S(1)} all-to-all(f32[1,1,384,768]{3,1,0,2:T(1,128)} %copy.132), channel_id=1, replica_groups=mesh['coil'=32,'slab'=16] {'slab'}, dimensions={2} | all-to-all | bytes 2359296 | tf_op jit(solution)/shard_map/all_to_all | solution.py:143
  549.8 34.2 %all_to_all.48 = f32[1,16,24,768]{3,2,0,1:T(8,128)S(1)} all-to-all(f32[1,16,24,768]{3,2,0,1:T(8,128)S(1)} %copy.135), channel_id=1, replica_groups=mesh['coil'=32,'slab'=16] {'slab'}, dimensions={1} | all-to-all | bytes 2359296 | tf_op jit(solution)/shard_map/all_to_all | solution.py:149
  584.0 2.3 convolution_bitcast_fusion.12
  586.3 2.3 convolution_bitcast_fusion.13
  592.3 147.3 %all-reduce.11.cloned.1.call-done = f32[1,192,384]{2,0,1:T(1,128)} async-done(((f32[1,192,384]{2,0,1:T(1,128)}), f32[1,192,384]{2,0,1:T(1,128)}) %all-reduce.11.cloned.1.call-update) | async-done | bytes 294928
  741.0 98.9 %psum.31 = f32[]{:T(128)} all-reduce(f32[]{:T(128)} %fusion.74), channel_id=1, replica_groups=mesh['coil'=32,'slab'=16] {'coil','slab'}, use_global_device_ids=true, to_apply=%region_9.10 | all-reduce | flops 1 | bytes 8 | tf_op jit(solution)/shard_map/psum | solution.py:157
  841.6 5.1 collective-permute-start
  846.7 1.9 collective-permute-start.1
  848.8 5.3 collective-permute-done.1
  854.3 4.0 collective-permute-start.3
  858.3 3.2 collective-permute-start.2
  862.5 1.5 fusion.194
  864.0 1.6 fusion.193
  865.6 4.4 concatenate.143
  870.9 1.7 concatenate.142
  873.3 1.7 concatenate.141
  877.1 1.9 collective-permute-start.4
  879.0 3.4 collective-permute-start.5
  882.4 3.6 collective-permute-done.5
  886.1 4.0 collective-permute-start.7
  890.1 4.5 collective-permute-start.6
  899.9 1.7 pad_slice_fusion.18
  901.6 2.0 pad_slice_fusion.19
  903.5 3.1 concatenate.146
  906.6 2.2 fusion.71
  908.8 2.7 concatenate.147
  911.5 2.4 convolution_add_fusion.1
  913.9 2.7 concatenate.148
  916.7 1.5 fusion.3
  918.8 1.9 collective-permute-start.8
  920.7 3.4 collective-permute-start.9
  924.1 4.0 collective-permute-done.9
  928.2 2.7 collective-permute-start.11
  930.9 5.8 collective-permute-start.10
  941.7 1.7 pad_slice_fusion
  943.4 2.0 pad_slice_fusion.1
  945.4 3.1 concatenate.151
  948.5 1.8 fusion.115
  950.3 2.7 concatenate.152
  953.0 1.9 convolution_add_fusion.5
  955.0 2.7 concatenate.153
  (141 shorter events, 50.6 us)
Async XLA Ops:
  8.7 18.6 %copy-start = (f32[1,1,192,384]{3,2,1,0:T(8,128)S(1)}, f32[1,1,192,384]{3,2,1,0:T(8,128)}, u32[]{:S(2)}) copy-start(f32[1,1,192,384]{3,2,1,0:T(8,128)} %param.9) | copy-start | bytes 884740
  8.8 18.0 %all-to-all-start = ((f32[32,1,6,384]{3,1,2,0:T(1,128)}), f32[32,1,6,384]{3,1,2,0:T(1,128)S(1)}, u32[]{:S(2)}, u32[]{:S(2)}) async-start(f32[32,1,6,384]{3,1,2,0:T(1,128)} %stack.10), calls=%async_computation | async-start | bytes 589824 | tf_op jit(solution)/shard_map/all_to_all | solution.py:15
  19.0 8.5 copy-start.11
  20.2 8.5 copy-start.13
  20.2 8.5 copy-start.15
  39.7 10.4 %copy-start.8 = (f32[16,24,384]{2,1,0:T(8,128)S(1)}, f32[16,24,384]{2,1,0:T(8,128)}, u32[]{:S(2)}) copy-start(f32[16,24,384]{2,1,0:T(8,128)} %param.10) | copy-start | bytes 1769476
  39.7 39.4 %all-to-all-start.1 = ((f32[1,1,384,768]{3,1,0,2:T(1,128)}), f32[1,1,384,768]{3,1,0,2:T(1,128)S(1)}, u32[]{:S(2)}, u32[]{:S(2)}) async-start(f32[1,1,384,768]{3,1,0,2:T(1,128)} %copy.123), calls=%async_computation.1 | async-start | bytes 2359296 | tf_op jit(solution)/shard_map/all_to_all | solution.py:143
  86.7 34.2 %all-to-all-start.2 = ((f32[1,16,24,768]{3,2,0,1:T(8,128)}), f32[1,16,24,768]{3,2,0,1:T(8,128)S(1)}, u32[]{:S(2)}, u32[]{:S(2)}) async-start(f32[1,16,24,768]{3,2,0,1:T(8,128)} %copy.127), calls=%async_computation.2 | async-start | bytes 2359296 | tf_op jit(solution)/shard_map/all_to_all | solution.py:149
  91.9 184.8 %all-reduce.9.cloned.1.call-start = ((), (), s32[]{:S(2)}) async-start(), calls=%async_computation.6 | async-start | bytes 589824
  125.6 1.0 copy-start.9
  129.3 610.4 %all-reduce.11.cloned.1.call-start = ((), (), s32[]{:S(2)}) async-start(), calls=%async_computation.7 | async-start | bytes 589824
  475.2 19.0 %copy-start.12 = (f32[192,384]{1,0:T(8,128)S(1)}, f32[192,384]{1,0:T(8,128)}, u32[]{:S(2)}) copy-start(f32[192,384]{1,0:T(8,128)} %copy-done.11) | copy-start | bytes 884740
  475.2 19.0 %copy-start.14 = (f32[192,384]{1,0:T(8,128)S(1)}, f32[192,384]{1,0:T(8,128)}, u32[]{:S(2)}) copy-start(f32[192,384]{1,0:T(8,128)} %copy-done.13) | copy-start | bytes 884740
  475.3 19.0 %copy-start.16 = (f32[192,384]{1,0:T(8,128)S(1)}, f32[192,384]{1,0:T(8,128)}, u32[]{:S(2)}) copy-start(f32[192,384]{1,0:T(8,128)} %copy-done.15) | copy-start | bytes 884740
  588.6 1.0 copy-start.10
  841.6 7.1 collective-permute-start
  846.7 7.5 collective-permute-start.1
  854.3 7.3 collective-permute-start.3
  858.3 4.0 collective-permute-start.2
  875.0 0.8 copy-start.18
  877.1 5.3 collective-permute-start.4
  879.0 6.9 collective-permute-start.5
  886.1 9.9 %collective-permute-start.7 = (bf16[1,8,12288]{2,1,0:T(8,128)(2,1)S(1)}, bf16[1,8,12288]{2,1,0:T(8,128)(2,1)S(1)}, u32[]{:S(2)}, u32[]{:S(2)}) collective-permute-start(bf16[1,8,12288]{2,1,0:T(8,128)(2,1)S(1)} %pad_maximum_fusion.6), channel_id=1, source_target_pairs={{1,0},{2,1},{3,2},{4,3},{5,4},{6,5},{7,6},{8,7},{9,8},{10,9},{11,1... | collective-permute-start | bytes 589832 | tf_op jit(solution)/shard_map/ppermute | solution.py:29
  890.1 7.1 collective-permute-start.6
  911.5 2.5 copy-start.1
  911.5 2.4 copy-start.2
  911.5 2.4 copy-start.3
  913.9 2.8 copy-start.7
  918.8 5.3 collective-permute-start.8
  920.7 7.4 collective-permute-start.9
  928.2 9.7 %collective-permute-start.11 = (bf16[1,8,12288]{2,1,0:T(8,128)(2,1)S(1)}, bf16[1,8,12288]{2,1,0:T(8,128)(2,1)S(1)}, u32[]{:S(2)}, u32[]{:S(2)}) collective-permute-start(bf16[1,8,12288]{2,1,0:T(8,128)(2,1)S(1)} %pad_maximum_fusion.7), channel_id=1, source_target_pairs={{1,0},{2,1},{3,2},{4,3},{5,4},{6,5},{7,6},{8,7},{9,8},{10,9},{11,1... | collective-permute-start | bytes 589832 | tf_op jit(solution)/shard_map/ppermute | solution.py:29
  930.9 8.1 collective-permute-start.10
  953.0 1.9 copy-start.4
  953.0 1.9 copy-start.5
  953.0 1.9 copy-start.6
  954.9 2.7 copy-start.17
Sparse Core Ops, SparseCore 0:
  129.4 147.2 all-reduce.8
  592.4 147.1 all-reduce.10
